TPU v7x, 32 devices: a whole 2x2x4 slice. The times are simulated.
32 devices in a mesh: replica: 2 (over core), shard: 16 (over z, y, x).
Axes of the slice: x: 2, y: 2, z: 4, core: 2. Of those that a mesh axis runs over, the one named last changes fastest.
Arguments:
- gradients: bfloat16 [2, 2, 16, 1024, 256], P('replica', None, None, 'shard'), may hold values from -36 to 36
- momentum: float32 [2, 16, 1024, 256], P('replica', None, 'shard'), may hold values from -3 to 3
- params: float32 [16, 1024, 256], P(None, ('shard', 'replica')), may hold values from -6 to 6
- outer_moment: float32 [16, 1024, 256], P(None, ('shard', 'replica')), may hold values from -2 to 2
- shadow: float32 [16, 1024, 256], P(None, ('shard', 'replica')), may hold values from -6 to 6
Outputs:
- new_params: float32 [16, 1024, 256], P(None, ('shard', 'replica'))
- new_outer_moment: float32 [16, 1024, 256], P(None, ('shard', 'replica'))
- new_shadow: float32 [16, 1024, 256], P(None, ('shard', 'replica'))
- new_momentum: float32 [2, 16, 1024, 256], P('replica', None, 'shard')
All inputs are finite; a program needn't handle non-finite values.
Results may differ from a plain program's by a relative error of at most 0.0085.
Values may be sent and summed in bfloat16 or wider, within the bound.
No kernel may reach another device: no remote copies, remote signals or barrier semaphores. Data moves between devices by JAX's collectives and lax.ppermute only.
A program may use at most 64 MiB of HBM per device.

v0:
```python
import math

import jax
import jax.numpy as jnp
from jax import lax
from jax.sharding import PartitionSpec as P

D = 1024
INNER = 2
NS_ITERS = 5


quintic_a = 3.4445
quintic_b = -4.775
quintic_c = 2.0315
inner_beta = 0.95
outer_mu = 0.9
outer_rate = 0.7
shadow_decay = 0.9


def newton_schulz(blocks):
    squares = jnp.sum(jnp.square(blocks.astype(jnp.float32)), axis=(1, 2), keepdims=True)
    current = (blocks.astype(jnp.float32) / (jnp.sqrt(squares) + 1e-07)).astype(jnp.bfloat16)
    for repeat in range(NS_ITERS):
        gram_block = jnp.einsum(
            "mdi,mdj->mij", current, current, preferred_element_type=jnp.float32
        ).astype(jnp.bfloat16)
        square = jnp.einsum(
            "mij,mjk->mik", gram_block, gram_block, preferred_element_type=jnp.float32
        )
        polynomial = (quintic_b * gram_block.astype(jnp.float32) + quintic_c * square).astype(
            jnp.bfloat16
        )
        product = jnp.einsum(
            "mdi,mij->mdj", current, polynomial, preferred_element_type=jnp.float32
        )
        current = (quintic_a * current.astype(jnp.float32) + product).astype(jnp.bfloat16)
    return current


def body(gradients, momentum, params, outer_moment, shadow):
    scale_step = 0.2 * math.sqrt(D)
    shard_count = lax.axis_size("shard")
    replica_count = lax.axis_size("replica")
    moment_now = momentum[0]
    updates = []
    for position in range(INNER):
        grad_now = gradients[0, position].astype(jnp.float32)
        moment_now = inner_beta * moment_now + grad_now
        updates.append((grad_now + inner_beta * moment_now).astype(jnp.bfloat16))
    owned_total = None
    for position in range(INNER):
        owned = lax.all_to_all(updates[position], "shard", split_axis=0, concat_axis=1, tiled=True)
        orthos = newton_schulz(owned)
        term = scale_step * orthos.astype(jnp.float32)
        owned_total = term if owned_total is None else owned_total + term
    mat_count = owned_total.shape[0]
    rows_each = owned_total.shape[1] // (shard_count * replica_count)
    width = owned_total.shape[2]
    grouped = owned_total.reshape((mat_count, shard_count, replica_count, rows_each, width))
    reduced = lax.psum_scatter(
        grouped.astype(jnp.bfloat16), "replica", scatter_dimension=2, tiled=True
    ).astype(jnp.float32)
    reduced = reduced.reshape((mat_count, shard_count, rows_each, width))
    placed = lax.all_to_all(
        reduced.astype(jnp.bfloat16), "shard", split_axis=1, concat_axis=0, tiled=True
    ).astype(reduced.dtype)
    summed = placed.reshape((mat_count * shard_count, rows_each, width))
    outer_delta = summed / replica_count
    new_outer = outer_mu * outer_moment + outer_delta
    new_params = params - outer_rate * (outer_delta + outer_mu * new_outer)
    new_shadow = shadow_decay * shadow + (1.0 - shadow_decay) * new_params
    return (new_params, new_outer, new_shadow, moment_now[None])


def solution(mesh):
    in_specs = (
        P("replica", None, None, "shard", None),
        P("replica", None, "shard", None),
        P(None, ("shard", "replica"), None),
        P(None, ("shard", "replica"), None),
        P(None, ("shard", "replica"), None),
    )
    out_specs = (
        P(None, ("shard", "replica"), None),
        P(None, ("shard", "replica"), None),
        P(None, ("shard", "replica"), None),
        P("replica", None, "shard", None),
    )
    return jax.shard_map(body, mesh=mesh, in_specs=in_specs, out_specs=out_specs, check_vma=False)
```

profile of v0, /device:TPU:0, one launch (start us, length us, event | category | flops | bytes accessed | tf_op | source)
XLA Modules:
  0.0 91.6 jit_solution(18344506976179949108)
XLA Ops:
  7.2 2.7 %fusion.46 = (bf16[16,64,256]{2,1,0:T(8,128)(2,1)S(1)}, bf16[16,64,256]{2,1,0:T(8,128)(2,1)}) fusion(f32[1,16,64,256]{3,2,1,0:T(8,128)} %param.6, bf16[1,2,16,64,256]{4,3,2,1,0:T(8,128)(2,1)} %param.5), kind=kLoop, calls=%fused_computation.84 | loop fusion | flops 2883584 | bytes 3145728 | tf_op jit(solution)/shard_map/convert_element_type | solution.py:51
  9.8 23.2 %all_to_all.12 = bf16[16,64,256]{2,1,0:T(8,128)(2,1)S(1)} all-to-all(bf16[16,64,256]{2,1,0:T(8,128)(2,1)S(1)} %get-tuple-element.7), channel_id=1, replica_groups=mesh['replica'=2,'shard'=16] {'shard'}, dimensions={0} | all-to-all | bytes 1048576 | tf_op jit(solution)/shard_map/all_to_all | solution.py:54
  33.0 3.9 %all-to-all-start.1 = ((bf16[16,64,256]{2,1,0:T(8,128)(2,1)}), bf16[16,64,256]{2,1,0:T(8,128)(2,1)S(1)}, u32[]{:S(2)}, u32[]{:S(2)}) async-start(bf16[16,64,256]{2,1,0:T(8,128)(2,1)} %get-tuple-element.8), calls=%async_computation.1 | async-start | bytes 1048576 | tf_op jit(solution)/shard_map/all_to_all | solution.py:54
  37.0 0.9 fusion.41
  39.1 0.5 fusion.4
  39.9 0.5 fusion.5
  40.8 0.5 fusion.6
  41.7 0.5 fusion.7
  42.6 8.8 %all-to-all-done.1 = bf16[16,64,256]{2,1,0:T(8,128)(2,1)S(1)} async-done(((bf16[16,64,256]{2,1,0:T(8,128)(2,1)}), bf16[16,64,256]{2,1,0:T(8,128)(2,1)S(1)}, u32[]{:S(2)}, u32[]{:S(2)}) %all-to-all-start.1) | async-done | bytes 524320 | tf_op jit(solution)/shard_map/all_to_all | solution.py:54
  51.4 0.9 fusion.43
  53.4 0.5 fusion.13
  54.3 0.5 fusion.14
  55.2 0.5 fusion.15
  55.7 0.3 convolution_convert_fusion.1
  56.1 0.5 fusion.16
  56.6 0.4 convolution_convert_fusion
  56.9 0.5 fusion.18
  57.5 0.5 fusion.12
  58.0 0.8 copy.10
  58.9 6.3 %reduce-scatter.2.cloned.1.call-done = bf16[1,16,1,32,256]{4,3,1,2,0:T(8,128)(2,1)} async-done(((bf16[1,16,2,32,256]{4,3,1,2,0:T(8,128)(2,1)}), bf16[1,16,1,32,256]{4,3,1,2,0:T(8,128)(2,1)}) %reduce-scatter.2.cloned.1.call-update) | async-done | bytes 262160 | tf_op jit(solution)/shard_map/reduce_scatter | solution.py:62
  65.2 6.7 %all-to-all-start.2 = ((bf16[1,16,32,256]{3,2,0,1:T(8,128)(2,1)}), bf16[1,16,32,256]{3,2,0,1:T(8,128)(2,1)S(1)}, u32[]{:S(2)}, u32[]{:S(2)}) async-start(bf16[1,16,32,256]{3,2,0,1:T(8,128)(2,1)} %bitcast.118), calls=%async_computation.3 | async-start | bytes 524288 | tf_op jit(solution)/shard_map/all_to_all | solution.py:66
  72.0 1.2 %fusion.49 = f32[1,16,64,256]{3,2,1,0:T(8,128)} fusion(f32[1,16,64,256]{3,2,1,0:T(8,128)S(1)} %copy-done, bf16[1,2,16,64,256]{4,3,2,1,0:T(8,128)(2,1)S(1)} %copy-done.1), kind=kLoop, calls=%fused_computation.87 | loop fusion | flops 1572864 | bytes 3145728 | tf_op jit(solution)/shard_map/add | solution.py:50
  73.2 9.1 %all-to-all-done.2 = bf16[1,16,32,256]{3,2,0,1:T(8,128)(2,1)S(1)} async-done(((bf16[1,16,32,256]{3,2,0,1:T(8,128)(2,1)}), bf16[1,16,32,256]{3,2,0,1:T(8,128)(2,1)S(1)}, u32[]{:S(2)}, u32[]{:S(2)}) %all-to-all-start.2) | async-done | bytes 262176 | tf_op jit(solution)/shard_map/all_to_all | solution.py:66
  82.4 2.4 %multiply_add_fusion = (f32[16,32,256]{2,1,0:T(8,128)}, f32[16,32,256]{2,1,0:T(8,128)}, f32[16,32,256]{2,1,0:T(8,128)}) fusion(f32[16,32,256]{2,1,0:T(8,128)S(1)} %copy-done.2, f32[16,32,256]{2,1,0:T(8,128)S(1)} %copy-done.3, bf16[1,16,32,256]{3,2,0,1:T(8,128)(2,1)S(1)} %all-to-all-done.2, f32[16,32,256]{2,1,0:T(8,128)} %param.8), kind=kLoop, calls=%fused_computation.94 | loop fusion | flops 1441792 | bytes 3407872 | tf_op jit(solution)/shard_map/add | solution.py:73
  (20 shorter events, 3.1 us)
Async XLA Ops:
  33.0 18.4 %all-to-all-start.1 = ((bf16[16,64,256]{2,1,0:T(8,128)(2,1)}), bf16[16,64,256]{2,1,0:T(8,128)(2,1)S(1)}, u32[]{:S(2)}, u32[]{:S(2)}) async-start(bf16[16,64,256]{2,1,0:T(8,128)(2,1)} %get-tuple-element.8), calls=%async_computation.1 | async-start | bytes 1048576 | tf_op jit(solution)/shard_map/all_to_all | solution.py:54
  37.0 28.2 %reduce-scatter.2.cloned.1.call-start = ((), (), s32[]{:S(2)}) async-start(), calls=%async_computation.4 | async-start | bytes 786432 | tf_op jit(solution)/shard_map/reduce_scatter | solution.py:62
  58.0 14.0 %copy-start = (f32[1,16,64,256]{3,2,1,0:T(8,128)S(1)}, f32[1,16,64,256]{3,2,1,0:T(8,128)}, u32[]{:S(2)}) copy-start(f32[1,16,64,256]{3,2,1,0:T(8,128)} %param.6) | copy-start | bytes 3145732
  58.0 14.0 %copy-start.1 = (bf16[1,2,16,64,256]{4,3,2,1,0:T(8,128)(2,1)S(1)}, bf16[1,2,16,64,256]{4,3,2,1,0:T(8,128)(2,1)}, u32[]{:S(2)}) copy-start(bf16[1,2,16,64,256]{4,3,2,1,0:T(8,128)(2,1)} %param.5) | copy-start | bytes 3145732
  65.2 17.1 %all-to-all-start.2 = ((bf16[1,16,32,256]{3,2,0,1:T(8,128)(2,1)}), bf16[1,16,32,256]{3,2,0,1:T(8,128)(2,1)S(1)}, u32[]{:S(2)}, u32[]{:S(2)}) async-start(bf16[1,16,32,256]{3,2,0,1:T(8,128)(2,1)} %bitcast.118), calls=%async_computation.3 | async-start | bytes 524288 | tf_op jit(solution)/shard_map/all_to_all | solution.py:66
  72.0 10.4 %copy-start.2 = (f32[16,32,256]{2,1,0:T(8,128)S(1)}, f32[16,32,256]{2,1,0:T(8,128)}, u32[]{:S(2)}) copy-start(f32[16,32,256]{2,1,0:T(8,128)} %param.9) | copy-start | bytes 1572868
  72.0 10.4 %copy-start.3 = (f32[16,32,256]{2,1,0:T(8,128)S(1)}, f32[16,32,256]{2,1,0:T(8,128)}, u32[]{:S(2)}) copy-start(f32[16,32,256]{2,1,0:T(8,128)} %param.7) | copy-start | bytes 1572868
Sparse Core Ops, SparseCore 0:
  59.0 6.1 reduce-scatter.1
where the time goes:
time: 92 us; the launch traced here: 91.6 us
  waiting for transfers between devices  24.3 us (26%)
  blocking collectives  23.2 us (25%)
  between operations  15.6 us (17%)
  starting transfers between devices  10.7 us (12%)
  matrix products  8.64 us (9%)
  other arithmetic  8.17 us (9%)
    all_to_all x1, blocking collectives, body(): lax.all_to_all(updates[position], 'shard', split_axis=0, concat_axis=1, t...  23.2 us
    all_to_all x1, waiting for transfers between devices, body(): lax.all_to_all(reduced.astype(jnp.bfloat16), 'shard', split_axis=1, conca...  9.13 us
    all_to_all x1, waiting for transfers between devices, body(): lax.all_to_all(updates[position], 'shard', split_axis=0, concat_axis=1, t...  8.85 us
    all_to_all x1, starting transfers between devices, body(): lax.all_to_all(reduced.astype(jnp.bfloat16), 'shard', split_axis=1, conca...  6.74 us
    reduce_scatter x1, waiting for transfers between devices, body(): lax.psum_scatter(grouped.astype(jnp.bfloat16), 'replica', scatter_dimensi...  6.34 us
    dot_general x10, matrix products, newton_schulz(): jnp.einsum('mdi,mij->mdj', current, polynomial, preferred_element_type=jn...  5.17 us
    all_to_all x1, starting transfers between devices, body(): lax.all_to_all(updates[position], 'shard', split_axis=0, concat_axis=1, t...  3.95 us
    dot_general x10, matrix products, newton_schulz(): jnp.einsum('mdi,mdj->mij', current, current, preferred_element_type=jnp.f...  3.47 us
  transfers between devices with their start and end apart: 3, of which 3 were waited for; matrix products, arithmetic and copies ran while one was open for 7% of the time, Pallas kernels for 0%

commit v1 on v0

v1 whole, which is shorter than its diff:
```python
import math

import jax
import jax.numpy as jnp
from jax import lax
from jax.sharding import PartitionSpec as P

NS_ITERS = 5

quintic_a = 3.4445
quintic_b = -4.775
quintic_c = 2.0315
inner_beta = 0.95
outer_mu = 0.9
outer_rate = 0.7
shadow_decay = 0.9


def newton_schulz(block):
    squares = jnp.sum(jnp.square(block.astype(jnp.float32)))
    current = (block.astype(jnp.float32) / (jnp.sqrt(squares) + 1e-07)).astype(jnp.bfloat16)
    for _ in range(NS_ITERS):
        gram = jnp.einsum(
            "di,dj->ij", current, current, preferred_element_type=jnp.float32
        ).astype(jnp.bfloat16)
        square = jnp.dot(gram, gram, preferred_element_type=jnp.float32)
        poly = (quintic_b * gram.astype(jnp.float32) + quintic_c * square).astype(jnp.bfloat16)
        product = jnp.dot(current, poly, preferred_element_type=jnp.float32)
        current = (quintic_a * current.astype(jnp.float32) + product).astype(jnp.bfloat16)
    return current


def body(gradients, momentum, params, outer_moment, shadow):
    shards = lax.axis_size("shard")
    replicas = lax.axis_size("replica")
    _, inner, mats, rows, width = gradients.shape
    owned = mats // shards
    total_rows = rows * shards
    rows_each = rows // replicas
    scale_step = 0.2 * math.sqrt(total_rows)

    moment = momentum[0]
    updates = []
    for k in range(inner):
        grad = gradients[0, k].astype(jnp.float32)
        moment = inner_beta * moment + grad
        updates.append((grad + inner_beta * moment).astype(jnp.bfloat16))
    stacked = jnp.stack(updates, axis=1)
    moved = lax.all_to_all(stacked, "shard", split_axis=0, concat_axis=0, tiled=True)
    moved = moved.reshape((shards, owned, inner, rows, width))

    totals = []
    for m in range(owned):
        total = None
        for k in range(inner):
            ortho = newton_schulz(moved[:, m, k].reshape((total_rows, width)))
            term = scale_step * ortho.astype(jnp.float32)
            total = term if total is None else total + term
        totals.append(total)
    total = jnp.stack(totals).reshape((owned, shards, replicas, rows_each, width))

    me = lax.axis_index("replica")
    summed = lax.dynamic_index_in_dim(total, me, 2, keepdims=False)
    for step in range(1, replicas):
        theirs = lax.dynamic_index_in_dim(total, (me + step) % replicas, 2, keepdims=False)
        got = lax.ppermute(
            theirs.astype(jnp.bfloat16),
            "replica",
            [(i, (i + step) % replicas) for i in range(replicas)],
        )
        summed = summed + got.astype(jnp.float32)
    placed = lax.all_to_all(
        summed.astype(jnp.bfloat16), "shard", split_axis=1, concat_axis=0, tiled=True
    )
    outer_delta = placed.reshape((mats, rows_each, width)).astype(jnp.float32) / replicas
    new_outer = outer_mu * outer_moment + outer_delta
    new_params = params - outer_rate * (outer_delta + outer_mu * new_outer)
    new_shadow = shadow_decay * shadow + (1.0 - shadow_decay) * new_params
    return (new_params, new_outer, new_shadow, moment[None])


def solution(mesh):
    rows = P(None, ("shard", "replica"), None)
    mine = P("replica", None, "shard", None)
    return jax.shard_map(
        body,
        mesh=mesh,
        in_specs=(P("replica", None, None, "shard", None), mine, rows, rows, rows),
        out_specs=(rows, rows, rows, mine),
        check_vma=False,
    )
```

time: 92 us -> 84.5 us (0.918)
  blocking collectives: 23.2 us -> 0 us
  between operations: 15.6 us -> 2.27 us
  waiting for transfers between devices: 24.3 us -> 34.9 us
  matrix products: 8.64 us -> 15.6 us
  local copies, waits for them, and re-layouts: 0.86 us -> 6.24 us
  starting transfers between devices: 10.7 us -> 14.3 us
  other arithmetic: 8.17 us -> 10.5 us
    all_to_all x1 -> x0, blocking collectives: 23.2 us -> none  [body(): lax.all_to_all(updates[position], 'shard', split_axis=0, concat_axis=1, t...]
    all_to_all x2, waiting for transfers between devices: 18 us -> 33.4 us  [the longest x1 24.4 us: body(): lax.all_to_all(stacked, 'shard', split_axis=0, concat_axis=0, tiled=True)]
    dot_general x20, matrix products: 8.64 us -> 15.6 us  [the longest x10 12.2 us: newton_schulz(): product = jnp.dot(current, poly, preferred_element_type=jnp.float32)]
    reduce_scatter x1 -> x0, waiting for transfers between devices: 6.34 us -> none  [body(): lax.psum_scatter(grouped.astype(jnp.bfloat16), 'replica', scatter_dimensi...]
    unnamed x8 -> x20, local copies, waits for them, and re-layouts: 0.03 us -> 3.88 us
    all_to_all x2, starting transfers between devices: 10.7 us -> 14.3 us  [the longest x1 8.39 us: body(): lax.all_to_all(stacked, 'shard', split_axis=0, concat_axis=0, tiled=True)]
    convert_element_type x3 -> x4, other arithmetic: 2.87 us -> 5.02 us  [the longest x2 2.16 us: body(): updates.append((grad + inner_beta * moment).astype(jnp.bfloat16))]
    ppermute x0 -> x1, waiting for transfers between devices: none -> 1.52 us  [body(): lax.ppermute(theirs.astype(jnp.bfloat16), 'replica', [(i, (i + step) % re...]
  transfers between devices with their start and end apart: 3 -> 3, of which waited for: 3 -> 3; matrix products, arithmetic and copies ran while one was open for 7% -> 1% of each run, Pallas kernels for 0% -> 0%
where the time goes in v1:
time: 84.5 us; the launch traced here: 83.9 us
  waiting for transfers between devices  34.9 us (41%)
  matrix products  15.6 us (18%)
  starting transfers between devices  14.3 us (17%)
  other arithmetic  10.5 us (12%)
  local copies, waits for them, and re-layouts  6.24 us (7%)
  between operations  2.27 us (3%)
    all_to_all x1, waiting for transfers between devices, body(): lax.all_to_all(stacked, 'shard', split_axis=0, concat_axis=0, tiled=True)  24.4 us
    dot_general x10, matrix products, newton_schulz(): product = jnp.dot(current, poly, preferred_element_type=jnp.float32)  12.2 us
    all_to_all x1, waiting for transfers between devices, body(): lax.all_to_all(summed.astype(jnp.bfloat16), 'shard', split_axis=1, concat...  8.93 us
    all_to_all x1, starting transfers between devices, body(): lax.all_to_all(stacked, 'shard', split_axis=0, concat_axis=0, tiled=True)  8.39 us
    all_to_all x1, starting transfers between devices, body(): lax.all_to_all(summed.astype(jnp.bfloat16), 'shard', split_axis=1, concat...  5.86 us
    unnamed x20, local copies, waits for them, and re-layouts  3.88 us
    dot_general x10, matrix products, newton_schulz(): jnp.einsum('di,dj->ij', current, current, preferred_element_type=jnp.floa...  3.45 us
    add x1, other arithmetic, body(): new_shadow = shadow_decay * shadow + (1.0 - shadow_decay) * new_params  2.35 us
  transfers between devices with their start and end apart: 3, of which 3 were waited for; matrix products, arithmetic and copies ran while one was open for 1% of the time, Pallas kernels for 0%

profile of v1, /device:TPU:0, one launch (start us, length us, event | category | flops | bytes accessed | tf_op | source)
XLA Modules:
  0.0 83.9 jit_solution(12345464679178923116)
XLA Ops:
  0.7 2.0 %fusion.51 = bf16[16,1,64,256]{3,2,1,0:T(8,128)(2,1)S(1)} fusion(f32[1,16,64,256]{3,2,1,0:T(8,128)} %param.6, bf16[1,2,16,64,256]{4,3,2,1,0:T(8,128)(2,1)} %param.5), kind=kLoop, calls=%fused_computation.89 | loop fusion | flops 2359296 | bytes 2621440 | tf_op jit(solution)/shard_map/convert_element_type | solution.py:47
  3.0 1.1 %pad_maximum_fusion = bf16[16,2,64,256]{3,2,1,0:T(8,128)(2,1)} fusion(bf16[16,1,64,256]{3,2,1,0:T(8,128)(2,1)S(1)} %fusion.51, bf16[16,1,64,256]{3,2,1,0:T(8,128)(2,1)S(1)} %fusion.52), kind=kLoop, calls=%fused_computation.90 | loop fusion | flops 524288 | bytes 2097152 | tf_op jit(solution)/shard_map/stack | solution.py:48
  4.1 8.4 %all-to-all-start = ((bf16[16,2,64,256]{3,2,1,0:T(8,128)(2,1)}), bf16[16,2,64,256]{3,2,1,0:T(8,128)(2,1)}, u32[]{:S(2)}, u32[]{:S(2)}) async-start(bf16[16,2,64,256]{3,2,1,0:T(8,128)(2,1)} %pad_maximum_fusion), calls=%async_computation | async-start | bytes 2097152 | tf_op jit(solution)/shard_map/all_to_all | solution.py:49
  12.5 24.4 %all-to-all-done = bf16[16,2,64,256]{3,2,1,0:T(8,128)(2,1)} async-done(((bf16[16,2,64,256]{3,2,1,0:T(8,128)(2,1)}), bf16[16,2,64,256]{3,2,1,0:T(8,128)(2,1)}, u32[]{:S(2)}, u32[]{:S(2)}) %all-to-all-start) | async-done | bytes 1048608 | tf_op jit(solution)/shard_map/all_to_all | solution.py:49
  36.9 1.3 %copy.17 = bf16[16,2,64,256]{3,2,0,1:T(8,128)(2,1)S(1)} copy(bf16[16,2,64,256]{3,2,1,0:T(8,128)(2,1)} %all-to-all-done) | data formatting | bytes 2097152 | tf_op jit(solution)/shard_map/all_to_all | solution.py:49
  38.2 0.9 %fusion.40 = (f32[]{:T(128)}, f32[]{:T(128)}) fusion(bf16[16,1,2,64,256]{4,3,0,2,1:T(8,128)(2,1)S(1)} %bitcast.151), kind=kLoop, calls=%fused_computation.78 | loop fusion | flops 1572862 | bytes 1048584 | tf_op jit(solution)/shard_map/reduce_sum | solution.py:20
  40.5 1.0 %fusion.41 = (bf16[16,1,1,64,256]{4,3,0,2,1:T(8,128)(2,1)S(1)}, bf16[16,1,1,64,256]{4,3,0,2,1:T(8,128)(2,1)}) fusion(f32[]{:T(128)S(6)} %add.149, bf16[16,1,2,64,256]{4,3,0,2,1:T(8,128)(2,1)S(1)} %bitcast.152, f32[]{:T(128)S(6)} %add.160), kind=kLoop, calls=%fused_computation.79 | loop fusion | flops 1572864 | bytes 2097160 | tf_op jit(solution)/shard_map/convert_element_type | solution.py:21
  42.3 1.7 %fusion.4 = bf16[1024,256]{1,0:T(8,128)(2,1)S(1)} fusion(bf16[1024,256]{1,0:T(8,128)(2,1)} %bitcast.156, bf16[256,256]{1,0:T(8,128)(2,1)S(1)} %fusion.28), kind=kOutput, calls=%fused_computation.22 | convolution fusion | flops 169148416 | bytes 1179648 | tf_op jit(solution)/shard_map/dot_general | solution.py:28
  45.3 0.5 fusion.6
  45.8 0.8 copy-done.8
  46.9 1.7 %fusion.7 = bf16[1024,256]{1,0:T(8,128)(2,1)S(1)} fusion(bf16[1024,256]{1,0:T(8,128)(2,1)} %copy-done.8, bf16[256,256]{1,0:T(8,128)(2,1)S(1)} %convolution_convert_fusion.5), kind=kOutput, calls=%fused_computation.25 | convolution fusion | flops 169148416 | bytes 1179648 | tf_op jit(solution)/shard_map/dot_general | solution.py:28
  52.0 0.5 fusion.14
  52.6 0.8 copy-done.9
  53.7 1.7 %fusion.15 = bf16[1024,256]{1,0:T(8,128)(2,1)S(1)} fusion(bf16[1024,256]{1,0:T(8,128)(2,1)} %copy-done.9, bf16[256,256]{1,0:T(8,128)(2,1)S(1)} %convolution_convert_fusion.1), kind=kOutput, calls=%fused_computation.33 | convolution fusion | flops 169148416 | bytes 1179648 | tf_op jit(solution)/shard_map/dot_general | solution.py:28
  55.4 0.8 copy-done.2
  56.6 1.7 %fusion.17 = f32[1024,256]{1,0:T(8,128)S(1)} fusion(bf16[1024,256]{1,0:T(8,128)(2,1)} %copy-done.2, bf16[256,256]{1,0:T(8,128)(2,1)S(1)} %convolution_convert_fusion), kind=kOutput, calls=%fused_computation.35 | convolution fusion | flops 169410560 | bytes 1703936 | tf_op jit(solution)/shard_map/dot_general | solution.py:28
  58.3 2.7 %fusion.11 = f32[1024,256]{1,0:T(8,128)} fusion(f32[1024,256]{1,0:T(8,128)S(1)} %fusion.17, bf16[1024,256]{1,0:T(8,128)(2,1)} %copy-done.5, bf16[256,256]{1,0:T(8,128)(2,1)S(1)} %convolution_convert_fusion.4), kind=kOutput, calls=%fused_computation.29 | convolution fusion | flops 169934848 | bytes 2752512 | tf_op jit(solution)/shard_map/dot_general | solution.py:28
  61.0 1.1 %fusion.58 = bf16[1,16,32,256]{3,2,0,1:T(8,128)(2,1)S(1)} fusion(f32[1,16,2,32,256]{4,3,2,1,0:T(8,128)} %bitcast.153, s32[]{:T(128)S(6)} %select_n.16), kind=kLoop, calls=%fused_computation.104 | loop fusion | bytes 524292 | tf_op jit(solution)/shard_map/convert_element_type | solution.py:67
  62.1 1.5 %collective-permute-done = bf16[1,16,32,256]{3,2,0,1:T(8,128)(2,1)S(1)} collective-permute-done((bf16[1,16,32,256]{3,2,0,1:T(8,128)(2,1)S(1)}, bf16[1,16,32,256]{3,2,0,1:T(8,128)(2,1)S(1)}, u32[]{:S(2)}, u32[]{:S(2)}) %collective-permute-start) | collective-permute-done | bytes 262176 | tf_op jit(solution)/shard_map/ppermute | solution.py:66
  63.7 1.8 %fusion.55 = bf16[1,16,32,256]{3,2,0,1:T(8,128)(2,1)} fusion(bf16[1,16,32,256]{3,2,0,1:T(8,128)(2,1)S(1)} %collective-permute-done, f32[1,16,2,32,256]{4,3,2,1,0:T(8,128)} %bitcast.154, s32[]{:T(128)S(6)} %select_n.14), kind=kLoop, calls=%fused_computation.99 | loop fusion | flops 393216 | bytes 1048580 | tf_op jit(solution)/shard_map/convert_element_type | solution.py:73
  65.5 5.9 %all-to-all-start.1 = ((bf16[1,16,32,256]{3,2,0,1:T(8,128)(2,1)}), bf16[1,16,32,256]{3,2,0,1:T(8,128)(2,1)S(1)}, u32[]{:S(2)}, u32[]{:S(2)}) async-start(bf16[1,16,32,256]{3,2,0,1:T(8,128)(2,1)} %fusion.55), calls=%async_computation.1 | async-start | bytes 524288 | tf_op jit(solution)/shard_map/all_to_all | solution.py:72
  71.4 1.2 %fusion.49 = f32[1,16,64,256]{3,2,1,0:T(8,128)} fusion(f32[1,16,64,256]{3,2,1,0:T(8,128)S(1)} %copy-done, bf16[1,2,16,64,256]{4,3,2,1,0:T(8,128)(2,1)S(1)} %copy-done.1), kind=kLoop, calls=%fused_computation.87 | loop fusion | flops 1572864 | bytes 3145728 | tf_op jit(solution)/shard_map/add | solution.py:46
  72.6 8.9 %all-to-all-done.1 = bf16[1,16,32,256]{3,2,0,1:T(8,128)(2,1)S(1)} async-done(((bf16[1,16,32,256]{3,2,0,1:T(8,128)(2,1)}), bf16[1,16,32,256]{3,2,0,1:T(8,128)(2,1)S(1)}, u32[]{:S(2)}, u32[]{:S(2)}) %all-to-all-start.1) | async-done | bytes 262176 | tf_op jit(solution)/shard_map/all_to_all | solution.py:72
  81.5 2.4 %multiply_add_fusion = (f32[16,32,256]{2,1,0:T(8,128)}, f32[16,32,256]{2,1,0:T(8,128)}, f32[16,32,256]{2,1,0:T(8,128)}) fusion(f32[16,32,256]{2,1,0:T(8,128)S(1)} %copy-done.3, f32[16,32,256]{2,1,0:T(8,128)S(1)} %copy-done.4, bf16[1,16,32,256]{3,2,0,1:T(8,128)(2,1)S(1)} %all-to-all-done.1, f32[16,32,256]{2,1,0:T(8,128)} %param.8), kind=kLoop, calls=%fused_computation.102 | loop fusion | flops 1441792 | bytes 3407872 | tf_op jit(solution)/shard_map/add | solution.py:78
  (32 shorter events, 6.8 us)
Async XLA Ops:
  0.6 2.0 %copy-start.1 = (bf16[1,2,16,64,256]{4,3,2,1,0:T(8,128)(2,1)S(1)}, bf16[1,2,16,64,256]{4,3,2,1,0:T(8,128)(2,1)}, u32[]{:S(2)}) copy-start(bf16[1,2,16,64,256]{4,3,2,1,0:T(8,128)(2,1)} %param.5) | copy-start | bytes 3145732
  0.6 2.2 %copy-start = (f32[1,16,64,256]{3,2,1,0:T(8,128)S(1)}, f32[1,16,64,256]{3,2,1,0:T(8,128)}, u32[]{:S(2)}) copy-start(f32[1,16,64,256]{3,2,1,0:T(8,128)} %param.6) | copy-start | bytes 3145732
  4.1 32.8 %all-to-all-start = ((bf16[16,2,64,256]{3,2,1,0:T(8,128)(2,1)}), bf16[16,2,64,256]{3,2,1,0:T(8,128)(2,1)}, u32[]{:S(2)}, u32[]{:S(2)}) async-start(bf16[16,2,64,256]{3,2,1,0:T(8,128)(2,1)} %pad_maximum_fusion), calls=%async_computation | async-start | bytes 2097152 | tf_op jit(solution)/shard_map/all_to_all | solution.py:49
  41.5 0.8 copy-start.7
  45.8 0.8 copy-start.8
  48.7 0.8 copy-start.5
  48.7 1.2 %copy-start.6 = (bf16[16,1,1,64,256]{4,3,0,2,1:T(8,128)(2,1)S(1)}, bf16[16,1,1,64,256]{4,3,0,2,1:T(8,128)(2,1)}, u32[]{:S(2)}) copy-start(bf16[16,1,1,64,256]{4,3,0,2,1:T(8,128)(2,1)} %get-tuple-element.10) | copy-start | bytes 1572868
  52.5 0.8 copy-start.9
  55.4 0.8 copy-start.2
  62.1 1.6 %collective-permute-start = (bf16[1,16,32,256]{3,2,0,1:T(8,128)(2,1)S(1)}, bf16[1,16,32,256]{3,2,0,1:T(8,128)(2,1)S(1)}, u32[]{:S(2)}, u32[]{:S(2)}) collective-permute-start(bf16[1,16,32,256]{3,2,0,1:T(8,128)(2,1)S(1)} %fusion.58), channel_id=1, source_target_pairs={{0,16},{16,0},{1,17},{17,1},{2,18},{18,2},{3,19},{19,3},{4,20},{20... | collective-permute-start | bytes 786440 | tf_op jit(solution)/shard_map/ppermute | solution.py:66
  65.5 16.0 %all-to-all-start.1 = ((bf16[1,16,32,256]{3,2,0,1:T(8,128)(2,1)}), bf16[1,16,32,256]{3,2,0,1:T(8,128)(2,1)S(1)}, u32[]{:S(2)}, u32[]{:S(2)}) async-start(bf16[1,16,32,256]{3,2,0,1:T(8,128)(2,1)} %fusion.55), calls=%async_computation.1 | async-start | bytes 524288 | tf_op jit(solution)/shard_map/all_to_all | solution.py:72
  71.4 10.2 %copy-start.3 = (f32[16,32,256]{2,1,0:T(8,128)S(1)}, f32[16,32,256]{2,1,0:T(8,128)}, u32[]{:S(2)}) copy-start(f32[16,32,256]{2,1,0:T(8,128)} %param.9) | copy-start | bytes 1572868
  71.4 10.2 %copy-start.4 = (f32[16,32,256]{2,1,0:T(8,128)S(1)}, f32[16,32,256]{2,1,0:T(8,128)}, u32[]{:S(2)}) copy-start(f32[16,32,256]{2,1,0:T(8,128)} %param.7) | copy-start | bytes 1572868

commit v2 on v1

v2 whole, which is shorter than its diff:
```python
import functools
import math

import jax
import jax.numpy as jnp
from jax import lax
from jax.experimental import pallas as pl
from jax.experimental.pallas import tpu as pltpu
from jax.sharding import PartitionSpec as P

NS_ITERS = 5

quintic_a = 3.4445
quintic_b = -4.775
quintic_c = 2.0315
inner_beta = 0.95
outer_mu = 0.9
outer_rate = 0.7
shadow_decay = 0.9

f32 = jnp.float32
bf16 = jnp.bfloat16
VMEM = pl.BlockSpec(memory_space=pltpu.VMEM)
SMEM = pl.BlockSpec(memory_space=pltpu.SMEM)


def gram_of(x):
    return lax.dot_general(x, x, (((0,), (0,)), ((), ())), preferred_element_type=f32)


def poly_of(gram):
    gram = gram.astype(bf16)
    square = jnp.dot(gram, gram, preferred_element_type=f32)
    return (quintic_b * gram.astype(f32) + quintic_c * square).astype(bf16)


def step_of(x, poly):
    return quintic_a * x.astype(f32) + jnp.dot(x, poly, preferred_element_type=f32)


def ns_kernel(me_ref, moved_ref, *refs, replicas):
    shards, inner, rows, width = moved_ref.shape
    outs, total_ref = refs[:replicas], refs[replicas]
    n_rows = shards * rows
    xs = [moved_ref[:, k].reshape(n_rows, width) for k in range(inner)]
    row = lax.broadcasted_iota(jnp.int32, (width, width), 0)
    diagonal = row == lax.broadcasted_iota(jnp.int32, (width, width), 1)
    grams = [gram_of(x) for x in xs]
    scales = []
    for gram in grams:
        squares = jnp.full((1, 1), jnp.sum(jnp.where(diagonal, gram, 0.0)), f32)
        scales.append(1.0 / (jnp.sqrt(squares) + 1e-07))
    polys = [poly_of(g * (s * s)) for g, s in zip(grams, scales)]
    xs = [(step_of(x, p) * s).astype(bf16) for x, p, s in zip(xs, polys, scales)]
    for _ in range(NS_ITERS - 2):
        polys = [poly_of(gram_of(x)) for x in xs]
        xs = [step_of(x, p).astype(bf16) for x, p in zip(xs, polys)]
    polys = [poly_of(gram_of(x)) for x in xs]
    total = None
    for x, p in zip(xs, polys):
        ortho = step_of(x, p)
        total = ortho if total is None else total + ortho
    total = (0.2 * math.sqrt(n_rows)) * total
    total_ref[...] = total.astype(bf16).reshape(total_ref.shape)
    me = me_ref[0]
    for s in range(shards):
        for d in range(replicas):
            outs[d][s] = total_ref[s * replicas + lax.rem(me + d, replicas)]


def orthogonal_parts(me, moved, replicas):
    shards, inner, rows, width = moved.shape
    rows_each = rows // replicas
    part = jax.ShapeDtypeStruct((shards, rows_each, width), bf16)
    return pl.pallas_call(
        functools.partial(ns_kernel, replicas=replicas),
        out_shape=[part] * replicas,
        in_specs=[SMEM, VMEM],
        out_specs=[VMEM] * replicas,
        scratch_shapes=[pltpu.VMEM((shards * replicas, rows_each, width), bf16)],
        compiler_params=pltpu.CompilerParams(vmem_limit_bytes=32 * 1024 * 1024),
        name="newton_schulz",
    )(me, moved)


def body(gradients, momentum, params, outer_moment, shadow):
    shards = lax.axis_size("shard")
    replicas = lax.axis_size("replica")
    _, inner, mats, rows, width = gradients.shape
    owned = mats // shards
    rows_each = rows // replicas

    moment = momentum[0]
    updates = []
    for k in range(inner):
        grad = gradients[0, k].astype(f32)
        moment = inner_beta * moment + grad
        updates.append((grad + inner_beta * moment).astype(bf16))
    stacked = jnp.stack(updates, axis=1)
    moved = lax.all_to_all(stacked, "shard", split_axis=0, concat_axis=0, tiled=True)
    moved = moved.reshape((shards, owned, inner, rows, width))

    me = lax.axis_index("replica").astype(jnp.int32)[None]
    summed = []
    for m in range(owned):
        parts = orthogonal_parts(me, moved[:, m], replicas)
        part = parts[0].astype(f32)
        for step in range(1, replicas):
            pairs = [(i, (i + step) % replicas) for i in range(replicas)]
            part = part + lax.ppermute(parts[step], "replica", pairs).astype(f32)
        summed.append(part.astype(bf16))
    summed = jnp.stack(summed)
    placed = lax.all_to_all(summed, "shard", split_axis=1, concat_axis=0, tiled=True)
    outer_delta = placed.reshape((mats, rows_each, width)).astype(f32) / replicas
    new_outer = outer_mu * outer_moment + outer_delta
    new_params = params - outer_rate * (outer_delta + outer_mu * new_outer)
    new_shadow = shadow_decay * shadow + (1.0 - shadow_decay) * new_params
    return (new_params, new_outer, new_shadow, moment[None])


def solution(mesh):
    rows = P(None, ("shard", "replica"), None)
    mine = P("replica", None, "shard", None)
    return jax.shard_map(
        body,
        mesh=mesh,
        in_specs=(P("replica", None, None, "shard", None), mine, rows, rows, rows),
        out_specs=(rows, rows, rows, mine),
        check_vma=False,
    )
```

time: 84.5 us -> 64.2 us (0.76)
  matrix products: 15.6 us -> 0 us
  Pallas kernels: 0 us -> 6.26 us
  local copies, waits for them, and re-layouts: 6.24 us -> 0.2 us
  other arithmetic: 10.5 us -> 7.58 us
  between operations: 2.27 us -> 0.71 us
    dot_general x20 -> x0, matrix products: 15.6 us -> none  [the longest x10 12.2 us: newton_schulz(): product = jnp.dot(current, poly, preferred_element_type=jnp.float32)]
    pallas_call x0 -> x1, Pallas kernels: none -> 6.26 us  [orthogonal_parts(): pl.pallas_call(functools.partial(ns_kernel, replicas=replicas), out_shape...]
    unnamed x20 -> x8, local copies, waits for them, and re-layouts: 3.88 us -> 0.2 us
    convert_element_type x4 -> x2, other arithmetic: 5.02 us -> 2.16 us  [body(): updates.append((grad + inner_beta * moment).astype(bf16))]
    all_to_all x1 -> x0, local copies, waits for them, and re-layouts: 1.29 us -> none  [body(): lax.all_to_all(stacked, 'shard', split_axis=0, concat_axis=0, tiled=True)]
    convert_element_type x1 -> x0, local copies, waits for them, and re-layouts: 1.07 us -> none  [body(): theirs.astype(jnp.bfloat16)]
    reduce_sum x1 -> x0, other arithmetic: 0.89 us -> none  [newton_schulz(): squares = jnp.sum(jnp.square(block.astype(jnp.float32)))]
  transfers between devices with their start and end apart: 3 -> 3, of which waited for: 3 -> 3; matrix products, arithmetic and copies ran while one was open for 1% -> 2% of each run, Pallas kernels for 0% -> 0%
where the time goes in v2:
time: 64.2 us; the launch traced here: 63.9 us
  waiting for transfers between devices  34.8 us (54%)
  starting transfers between devices  14.3 us (22%)
  other arithmetic  7.58 us (12%)
  Pallas kernels  6.26 us (10%)
  between operations  0.71 us (1%)
    all_to_all x1, waiting for transfers between devices, body(): lax.all_to_all(stacked, 'shard', split_axis=0, concat_axis=0, tiled=True)  24.4 us
    all_to_all x1, waiting for transfers between devices, body(): lax.all_to_all(summed, 'shard', split_axis=1, concat_axis=0, tiled=True)  8.93 us
    all_to_all x1, starting transfers between devices, body(): lax.all_to_all(stacked, 'shard', split_axis=0, concat_axis=0, tiled=True)  8.34 us
    pallas_call x1, Pallas kernels, orthogonal_parts(): pl.pallas_call(functools.partial(ns_kernel, replicas=replicas), out_shape...  6.26 us
    all_to_all x1, starting transfers between devices, body(): lax.all_to_all(summed, 'shard', split_axis=1, concat_axis=0, tiled=True)  5.88 us
    add x1, other arithmetic, body(): new_shadow = shadow_decay * shadow + (1.0 - shadow_decay) * new_params  2.35 us
    convert_element_type x2, other arithmetic, body(): updates.append((grad + inner_beta * moment).astype(bf16))  2.16 us
    ppermute x1, waiting for transfers between devices, body(): part = part + lax.ppermute(parts[step], 'replica', pairs).astype(f32)  1.52 us
  transfers between devices with their start and end apart: 3, of which 3 were waited for; matrix products, arithmetic and copies ran while one was open for 2% of the time, Pallas kernels for 0%

profile of v2, /device:TPU:0, one launch (start us, length us, event | category | flops | bytes accessed | tf_op | source)
XLA Modules:
  0.0 63.9 jit_solution(3041200509673687485)
XLA Ops:
  0.6 0.0 copy-start.1
  0.6 0.0 copy-start
  0.7 2.0 %fusion.11 = bf16[16,1,64,256]{3,2,1,0:T(8,128)(2,1)S(1)} fusion(f32[1,16,64,256]{3,2,1,0:T(8,128)} %param.6, bf16[1,2,16,64,256]{4,3,2,1,0:T(8,128)(2,1)} %param.5), kind=kLoop, calls=%fused_computation.15 | loop fusion | flops 2359296 | bytes 2621440 | tf_op jit(solution)/shard_map/convert_element_type | solution.py:98
  2.6 0.0 copy-done.1
  2.6 0.2 copy-done
  2.8 0.2 fusion.12
  3.0 1.1 %pad_maximum_fusion = bf16[16,2,64,256]{3,2,1,0:T(8,128)(2,1)} fusion(bf16[16,1,64,256]{3,2,1,0:T(8,128)(2,1)S(1)} %fusion.11, bf16[16,1,64,256]{3,2,1,0:T(8,128)(2,1)S(1)} %fusion.12), kind=kLoop, calls=%fused_computation.16 | loop fusion | flops 524288 | bytes 2097152 | tf_op jit(solution)/shard_map/stack | solution.py:99
  4.1 8.3 %all-to-all-start = ((bf16[16,2,64,256]{3,2,1,0:T(8,128)(2,1)}), bf16[16,2,64,256]{3,2,1,0:T(8,128)(2,1)S(1)}, u32[]{:S(2)}, u32[]{:S(2)}) async-start(bf16[16,2,64,256]{3,2,1,0:T(8,128)(2,1)} %pad_maximum_fusion), calls=%async_computation | async-start | bytes 2097152 | tf_op jit(solution)/shard_map/all_to_all | solution.py:100
  12.4 24.4 %all-to-all-done.moved_ref = bf16[16,2,64,256]{3,2,1,0:T(8,128)(2,1)S(1)} async-done(((bf16[16,2,64,256]{3,2,1,0:T(8,128)(2,1)}), bf16[16,2,64,256]{3,2,1,0:T(8,128)(2,1)S(1)}, u32[]{:S(2)}, u32[]{:S(2)}) %all-to-all-start) | async-done | bytes 1048608 | tf_op jit(solution)/shard_map/all_to_all | solution.py:100
  36.8 6.3 %newton_schulz.1 = (bf16[16,32,256]{2,1,0:T(8,128)(2,1)S(1)}, bf16[16,32,256]{2,1,0:T(8,128)(2,1)S(1)}) custom-call(s32[1]{0:T(128)} %bitcast.me_ref, bf16[16,2,64,256]{3,2,1,0:T(8,128)(2,1)S(1)} %all-to-all-done.moved_ref), custom_call_target="tpu_custom_call" | custom-call | tf_op jit(solution)/shard_map/newton_schulz/pallas_call | solution.py:75
  43.1 0.1 collective-permute-start
  43.2 1.5 %collective-permute-done = bf16[16,32,256]{2,1,0:T(8,128)(2,1)S(1)} collective-permute-done((bf16[16,32,256]{2,1,0:T(8,128)(2,1)S(1)}, bf16[16,32,256]{2,1,0:T(8,128)(2,1)S(1)}, u32[]{:S(2)}, u32[]{:S(2)}) %collective-permute-start) | collective-permute-done | bytes 262176 | tf_op jit(solution)/shard_map/ppermute | solution.py:110
  44.7 0.8 %fusion.15 = bf16[1,16,32,256]{3,2,0,1:T(8,128)(2,1)} fusion(bf16[16,32,256]{2,1,0:T(8,128)(2,1)S(1)} %collective-permute-done, bf16[16,32,256]{2,1,0:T(8,128)(2,1)S(1)} %get-tuple-element.6), kind=kLoop, calls=%fused_computation.25 | loop fusion | flops 524288 | bytes 786432 | tf_op jit(solution)/shard_map/stack | solution.py:112
  45.5 5.9 %all-to-all-start.1 = ((bf16[1,16,32,256]{3,2,0,1:T(8,128)(2,1)}), bf16[1,16,32,256]{3,2,0,1:T(8,128)(2,1)S(1)}, u32[]{:S(2)}, u32[]{:S(2)}) async-start(bf16[1,16,32,256]{3,2,0,1:T(8,128)(2,1)} %fusion.15), calls=%async_computation.1 | async-start | bytes 524288 | tf_op jit(solution)/shard_map/all_to_all | solution.py:113
  51.4 0.0 copy-start.2
  51.4 0.0 copy-start.3
  51.4 1.2 %fusion.9 = f32[1,16,64,256]{3,2,1,0:T(8,128)} fusion(f32[1,16,64,256]{3,2,1,0:T(8,128)S(1)} %copy-done, bf16[1,2,16,64,256]{4,3,2,1,0:T(8,128)(2,1)S(1)} %copy-done.1), kind=kLoop, calls=%fused_computation.13 | loop fusion | flops 1572864 | bytes 3145728 | tf_op jit(solution)/shard_map/add | solution.py:97
  52.6 8.9 %all-to-all-done.1 = bf16[1,16,32,256]{3,2,0,1:T(8,128)(2,1)S(1)} async-done(((bf16[1,16,32,256]{3,2,0,1:T(8,128)(2,1)}), bf16[1,16,32,256]{3,2,0,1:T(8,128)(2,1)S(1)}, u32[]{:S(2)}, u32[]{:S(2)}) %all-to-all-start.1) | async-done | bytes 262176 | tf_op jit(solution)/shard_map/all_to_all | solution.py:113
  61.5 0.0 copy-done.2
  61.5 0.0 copy-done.3
  61.5 2.4 %multiply_add_fusion = (f32[16,32,256]{2,1,0:T(8,128)}, f32[16,32,256]{2,1,0:T(8,128)}, f32[16,32,256]{2,1,0:T(8,128)}) fusion(f32[16,32,256]{2,1,0:T(8,128)S(1)} %copy-done.2, f32[16,32,256]{2,1,0:T(8,128)S(1)} %copy-done.3, bf16[1,16,32,256]{3,2,0,1:T(8,128)(2,1)S(1)} %all-to-all-done.1, f32[16,32,256]{2,1,0:T(8,128)} %param.8), kind=kLoop, calls=%fused_computation.22 | loop fusion | flops 1441792 | bytes 3407872 | tf_op jit(solution)/shard_map/add | solution.py:117
Async XLA Ops:
  0.6 2.0 %copy-start.1 = (bf16[1,2,16,64,256]{4,3,2,1,0:T(8,128)(2,1)S(1)}, bf16[1,2,16,64,256]{4,3,2,1,0:T(8,128)(2,1)}, u32[]{:S(2)}) copy-start(bf16[1,2,16,64,256]{4,3,2,1,0:T(8,128)(2,1)} %param.5) | copy-start | bytes 3145732
  0.6 2.2 %copy-start = (f32[1,16,64,256]{3,2,1,0:T(8,128)S(1)}, f32[1,16,64,256]{3,2,1,0:T(8,128)}, u32[]{:S(2)}) copy-start(f32[1,16,64,256]{3,2,1,0:T(8,128)} %param.6) | copy-start | bytes 3145732
  4.1 32.7 %all-to-all-start = ((bf16[16,2,64,256]{3,2,1,0:T(8,128)(2,1)}), bf16[16,2,64,256]{3,2,1,0:T(8,128)(2,1)S(1)}, u32[]{:S(2)}, u32[]{:S(2)}) async-start(bf16[16,2,64,256]{3,2,1,0:T(8,128)(2,1)} %pad_maximum_fusion), calls=%async_computation | async-start | bytes 2097152 | tf_op jit(solution)/shard_map/all_to_all | solution.py:100
  43.1 1.6 %collective-permute-start = (bf16[16,32,256]{2,1,0:T(8,128)(2,1)S(1)}, bf16[16,32,256]{2,1,0:T(8,128)(2,1)S(1)}, u32[]{:S(2)}, u32[]{:S(2)}) collective-permute-start(bf16[16,32,256]{2,1,0:T(8,128)(2,1)S(1)} %get-tuple-element.7), channel_id=1, source_target_pairs={{0,16},{16,0},{1,17},{17,1},{2,18},{18,2},{3,19},{19,3},{4,20},{20... | collective-permute-start | bytes 786440 | tf_op jit(solution)/shard_map/ppermute | solution.py:110
  45.5 16.1 %all-to-all-start.1 = ((bf16[1,16,32,256]{3,2,0,1:T(8,128)(2,1)}), bf16[1,16,32,256]{3,2,0,1:T(8,128)(2,1)S(1)}, u32[]{:S(2)}, u32[]{:S(2)}) async-start(bf16[1,16,32,256]{3,2,0,1:T(8,128)(2,1)} %fusion.15), calls=%async_computation.1 | async-start | bytes 524288 | tf_op jit(solution)/shard_map/all_to_all | solution.py:113
  51.4 10.2 %copy-start.2 = (f32[16,32,256]{2,1,0:T(8,128)S(1)}, f32[16,32,256]{2,1,0:T(8,128)}, u32[]{:S(2)}) copy-start(f32[16,32,256]{2,1,0:T(8,128)} %param.9) | copy-start | bytes 1572868
  51.4 10.2 %copy-start.3 = (f32[16,32,256]{2,1,0:T(8,128)S(1)}, f32[16,32,256]{2,1,0:T(8,128)}, u32[]{:S(2)}) copy-start(f32[16,32,256]{2,1,0:T(8,128)} %param.7) | copy-start | bytes 1572868
